TPU v7x, 32 devices: a whole 2x2x4 slice. The times are simulated.
32 devices in a mesh: groups: 2 (over x), month: 16 (over z, y, core).
Axes of the slice: x: 2, y: 2, z: 4, core: 2. Of those that a mesh axis runs over, the one named last changes fastest.
Arguments:
- shocks: float32 [512, 4096], P('month', 'groups'), parts along dimension 1, may hold values from -6 to 6
- long_mean: float32 [512], P('month'), may hold values from 0 to 0.08
- reversion: float32 [4096], P('groups'), parts along dimension 0, may hold values from 0.1 to 1
- volatility: float32 [4096], P('groups'), parts along dimension 0, may hold values from 0.004 to 0.015
- start_rate: float32 [4096], P('groups'), parts along dimension 0, may hold values from 0 to 0.06
- cash_flows: bfloat16 [3, 512, 24576], P(None, 'month', 'groups'), parts along dimension 2, may hold values from -0.5 to 0.5
Outputs:
- present: bfloat16 [3, 24576, 2048], P(None, ('groups', 'month')), parts along dimension 1
There are 2 independent parts, one for each index of `groups`. A program takes and returns all parts, laid end to end along the dimension named above; an argument that names none is the same for every part. Nothing has to cross between parts.
All inputs are finite; a program needn't handle non-finite values.
Results may differ from a plain program's by a relative error of at most 0.0049.
Values may be sent and summed in bfloat16 or wider, within the bound.
A program may use at most 192 MiB of HBM per device.

v0:
```python
import math
import jax
import jax.numpy as jnp
from jax import lax
from jax.sharding import PartitionSpec as P

month_step = 1.0 / 12.0
root_step = math.sqrt(1.0 / 12.0)
risk_price = 0.15
price_scale = risk_price * math.sqrt(12.0)
price_drift = 0.5 * risk_price * risk_price


def prefix(part, axis, combine, identity):
    place = lax.axis_index(axis)
    gathered = jax.tree.map(lambda a: lax.all_gather(a, axis), part)
    state = jax.tree.map(lambda a, e: jnp.zeros_like(a) + jnp.asarray(e, a.dtype), part, identity)

    def one(hop, state):
        return combine(
            state, jax.tree.map(lambda a: lax.dynamic_index_in_dim(a, hop, 0, False), gathered)
        )

    return lax.fori_loop(0, place, one, state)


def compose(earlier, later):
    return (
        later[0] * earlier[0],
        later[0] * earlier[1] + later[1],
        earlier[2] + later[2] * earlier[0],
        earlier[3] + later[3] + later[2] * earlier[1],
    )


def month_maps(shocks, long_mean, reversion, volatility):
    persist = 1.0 - reversion * month_step
    drive = (reversion * month_step)[None, :] * long_mean[:, None] + (volatility * root_step)[
        None, :
    ] * shocks
    factor = jnp.broadcast_to(persist[None, :], drive.shape)
    extra = drive + price_scale * shocks + price_drift
    return lax.associative_scan(compose, (factor, drive, factor, extra), axis=0)


def discount_from(maps, rate_in, total_in):
    total = total_in[None, :] + maps[2] * rate_in[None, :] + maps[3]
    return jnp.exp(-month_step * total).astype(jnp.bfloat16)


def time_discount(shocks, long_mean, reversion, volatility, start_rate):
    maps = month_maps(shocks, long_mean, reversion, volatility)
    block = tuple((member[-1] for member in maps))
    unit_row = jnp.ones_like(start_rate)
    zero_row = jnp.zeros_like(start_rate)
    before = prefix(block, "month", compose, (unit_row, zero_row, zero_row, zero_row))
    rate_in = before[0] * start_rate + before[1]
    total_in = before[2] * start_rate + before[3]
    return discount_from(maps, rate_in, total_in)


def contract(flows, discount):
    blocks = []
    for leg_index in range(flows.shape[0]):
        value = lax.dot_general(
            flows[leg_index], discount, (((0,), (0,)), ((), ())), preferred_element_type=jnp.float32
        )
        blocks.append(value.astype(jnp.bfloat16))
    return jnp.stack(blocks)


def local(shocks, long_mean, reversion, volatility, start_rate, cash_flows):
    own_flows = lax.all_to_all(cash_flows, "month", split_axis=2, concat_axis=1, tiled=True)
    discount = time_discount(shocks, long_mean, reversion, volatility, start_rate)
    every_month = lax.all_gather(discount, "month", axis=0, tiled=True)
    return contract(own_flows, every_month)


def solution(mesh):
    placed = (
        P("month", "groups"),
        P("month"),
        P("groups"),
        P("groups"),
        P("groups"),
        P(None, "month", "groups"),
    )
    return jax.shard_map(
        local,
        mesh=mesh,
        in_specs=placed,
        out_specs=P(None, ("groups", "month"), None),
        check_vma=False,
    )
```

profile of v0, /device:TPU:0, one launch (start us, length us, event | category | flops | bytes accessed | tf_op | source)
XLA Modules:
  0.0 273.4 jit_solution(5829222085009719674)
XLA Ops:
  6.5 15.3 %copy.13 = bf16[3,32,12288]{1,0,2:T(4,128)(2,1)} copy(bf16[3,32,12288]{2,1,0:T(8,128)(2,1)} %param.13) | data formatting | bytes 4718592 | tf_op args[5]
  21.8 15.7 %reshape.39 = bf16[16,2,36864]{2,1,0:T(2,128)(2,1)} reshape(bf16[12288,3,32]{2,1,0:T(4,128)(2,1)} %bitcast.69) | data formatting | bytes 4718592
  37.5 7.6 %all-to-all-start = ((bf16[16,2,36864]{2,1,0:T(2,128)(2,1)}), bf16[16,2,36864]{2,1,0:T(2,128)(2,1)S(1)}, u32[]{:S(2)}, u32[]{:S(2)}) async-start(bf16[16,2,36864]{2,1,0:T(2,128)(2,1)} %reshape.39), calls=%async_computation | async-start | bytes 4718592 | tf_op jit(solution)/shard_map/all_to_all | solution.py:73
  45.1 0.0 all-gather.6.cloned.1.call-start
  45.2 0.1 multiply_add_fusion.3
  45.4 0.6 slice.387
  46.0 0.1 slice.349
  46.2 0.6 slice.388
  46.9 0.6 slice.363
  48.1 0.1 fusion.21
  48.8 0.1 multiply_add_fusion.9
  49.2 0.6 add.336
  49.9 0.7 multiply_add_fusion.6
  50.6 0.7 pad_maximum_fusion.6
  51.3 0.7 pad_maximum_fusion.8
  52.2 0.7 add.363
  52.9 0.7 add.309
  53.5 0.7 add_multiply_fusion.1
  54.2 0.9 pad_maximum_fusion.7
  55.1 0.9 pad.153
  56.0 0.9 add_add_fusion.2
  57.1 43.2 %all-gather.2 = f32[16,1,2048]{2,1,0:T(1,128)S(1)} all-gather(f32[1,1,2048]{2,1,0:T(1,128)S(1)} %add_bitcast_fusion.1), channel_id=1, replica_groups=mesh['groups'=2,'month'=16] {'month'}, dimensions={0}, use_global_device_ids=true | all-gather | bytes 139264 | tf_op jit(solution)/shard_map/all_gather | solution.py:16
  100.3 0.7 copy.29
  101.0 0.7 pad_maximum_fusion.4
  101.8 1.0 pad.165
  102.8 28.5 %all-gather.3 = f32[16,1,2048]{2,1,0:T(1,128)S(1)} all-gather(f32[1,1,2048]{2,1,0:T(1,128)S(1)} %add_bitcast_fusion), channel_id=1, replica_groups=mesh['groups'=2,'month'=16] {'month'}, dimensions={0}, use_global_device_ids=true | all-gather | bytes 139264 | tf_op jit(solution)/shard_map/all_gather | solution.py:16
  131.3 0.7 copy.28
  132.0 2.3 pad.299
  134.4 1.4 pad.301
  135.8 0.9 add_bitcast_fusion.2
  136.7 17.8 %all-gather.1 = f32[16,1,2048]{2,1,0:T(1,128)S(1)} all-gather(f32[1,1,2048]{2,1,0:T(1,128)S(1)} %get-tuple-element.132), channel_id=1, replica_groups=mesh['groups'=2,'month'=16] {'month'}, dimensions={0}, use_global_device_ids=true | all-gather | bytes 139264 | tf_op jit(solution)/shard_map/all_gather | solution.py:16
  154.5 0.7 copy.30
  155.2 19.1 %all-gather = f32[16,1,2048]{2,1,0:T(1,128)S(1)} all-gather(f32[1,1,2048]{2,1,0:T(1,128)S(1)} %get-tuple-element.133), channel_id=1, replica_groups=mesh['groups'=2,'month'=16] {'month'}, dimensions={0}, use_global_device_ids=true | all-gather | bytes 139264 | tf_op jit(solution)/shard_map/all_gather | solution.py:16
  174.3 0.7 copy.31
  175.0 0.2 while.16
  175.2 0.7 exponential_convert_fusion
  176.0 11.8 %reshape.40 = bf16[12288,3,32]{2,1,0:T(4,128)(2,1)} reshape(bf16[16,2,36864]{2,1,0:T(2,128)(2,1)S(1)} %all-to-all-done) | data formatting | bytes 4718592
  187.7 11.7 %copy.19 = bf16[3,32,16,768]{3,2,1,0:T(8,128)(2,1)S(1)} copy(bf16[3,32,16,768]{1,0,3,2:T(4,128)(2,1)} %bitcast.68) | data formatting | bytes 4718592 | tf_op jit(solution)/shard_map/all_to_all | solution.py:73
  199.4 0.2 fusion.18
  199.6 0.2 copy.15
  199.8 0.2 copy.17
  200.1 0.2 copy.16
  200.3 41.7 %all-gather.6.cloned.1.call-done = bf16[512,2048]{1,0:T(8,128)(2,1)} async-done(((bf16[32,2048]{1,0:T(8,128)(2,1)}), bf16[512,2048]{1,0:T(8,128)(2,1)}) %all-gather.6.cloned.1.call-update) | async-done | bytes 2097168 | tf_op jit(solution)/shard_map/all_gather | solution.py:75
  242.0 3.6 %fusion.1 = bf16[1,768,2048]{1,2,0:T(8,128)(2,1)S(1)} fusion(bf16[512,2048]{1,0:T(8,128)(2,1)} %all-gather.6.cloned.1.call-done, bf16[512,768]{1,0:T(8,128)(2,1)S(1)} %bitcast.77), kind=kOutput, calls=%fused_computation.12 | convolution fusion | flops 1612185600 | bytes 6029312 | tf_op jit(solution)/shard_map/dot_general | solution.py:65
  245.6 1.9 fusion.2
  247.5 1.9 fusion
  249.4 4.6 %pad_maximum_fusion = bf16[3,768,2048]{1,2,0:T(8,128)(2,1)} fusion(bf16[1,768,2048]{1,2,0:T(8,128)(2,1)S(1)} %fusion.2, bf16[1,768,2048]{1,2,0:T(8,128)(2,1)S(1)} %fusion.1, bf16[1,768,2048]{1,2,0:T(8,128)(2,1)S(1)} %fusion), kind=kLoop, calls=%fused_computation.7 | loop fusion | flops 9437184 | bytes 18874368 | tf_op jit(solution)/shard_map/stack | solution.py:69
  253.9 12.6 %copy.18 = bf16[3,768,2048]{2,1,0:T(8,128)(2,1)} copy(bf16[3,768,2048]{1,2,0:T(8,128)(2,1)} %pad_maximum_fusion) | data formatting | bytes 18874368 | tf_op jit(solution)/shard_map/stack | solution.py:69
  (99 shorter events, 2.0 us)
Async XLA Ops:
  37.5 7.6 %copy-start.2 = (f32[2048]{0:T(1024)S(1)}, f32[2048]{0:T(1024)}, u32[]{:S(2)}) copy-start(f32[2048]{0:T(1024)} %param.10) | copy-start | bytes 24580
  37.5 7.6 %copy-start.3 = (f32[2048]{0:T(1024)S(1)}, f32[2048]{0:T(1024)}, u32[]{:S(2)}) copy-start(f32[2048]{0:T(1024)} %param.11) | copy-start | bytes 24580
  37.5 7.7 %copy-start = (f32[32,2048]{1,0:T(8,128)S(1)}, f32[32,2048]{1,0:T(8,128)}, u32[]{:S(2)}) copy-start(f32[32,2048]{1,0:T(8,128)} %param.8) | copy-start | bytes 786436
  37.5 7.7 %copy-start.4 = (f32[32]{0:T(128)S(1)}, f32[32]{0:T(128)}, u32[]{:S(2)}) copy-start(f32[32]{0:T(128)} %param.9) | copy-start | bytes 388
  37.5 138.4 %all-to-all-start = ((bf16[16,2,36864]{2,1,0:T(2,128)(2,1)}), bf16[16,2,36864]{2,1,0:T(2,128)(2,1)S(1)}, u32[]{:S(2)}, u32[]{:S(2)}) async-start(bf16[16,2,36864]{2,1,0:T(2,128)(2,1)} %reshape.39), calls=%async_computation | async-start | bytes 4718592 | tf_op jit(solution)/shard_map/all_to_all | solution.py:73
  45.1 196.9 %all-gather.6.cloned.1.call-start = ((), (), s32[]{:S(2)}) async-start(), calls=%async_computation.1 | async-start | bytes 2228224 | tf_op jit(solution)/shard_map/all_gather | solution.py:75
  56.0 119.2 %copy-start.1 = (f32[2048]{0:T(1024)S(1)}, f32[2048]{0:T(1024)}, u32[]{:S(2)}) copy-start(f32[2048]{0:T(1024)} %param.12) | copy-start | bytes 24580
  242.0 3.6 %copy-start.5 = (bf16[512,2048]{1,0:T(8,128)(2,1)S(1)}, bf16[512,2048]{1,0:T(8,128)(2,1)}, u32[]{:S(2)}) copy-start(bf16[512,2048]{1,0:T(8,128)(2,1)} %all-gather.6.cloned.1.call-done) | copy-start | bytes 6291460
Sparse Core Ops, SparseCore 0:
  176.1 65.8 all-gather.5
where the time goes:
time: 277 us; the launch traced here: 273 us
  blocking collectives  109 us (39%)
  local copies, waits for them, and re-layouts  79.5 us (29%)
  waiting for transfers between devices  41.7 us (15%)
  other arithmetic  14.3 us (5%)
  between operations  14.1 us (5%)
  starting transfers between devices  7.6 us (3%)
  matrix products  7.31 us (3%)
    all_gather x4, blocking collectives, prefix(): gathered = jax.tree.map(lambda a: lax.all_gather(a, axis), part)  109 us
    unnamed x21, local copies, waits for them, and re-layouts  49.3 us
    all_gather x1, waiting for transfers between devices, local(): every_month = lax.all_gather(discount, 'month', axis=0, tiled=True)  41.7 us
    another operation x1, local copies, waits for them, and re-layouts, contract(): return jnp.stack(blocks)  12.6 us
    all_to_all x1, local copies, waits for them, and re-layouts, local(): lax.all_to_all(cash_flows, 'month', split_axis=2, concat_axis=1, tiled=True)  11.7 us
    all_to_all x1, starting transfers between devices, local(): lax.all_to_all(cash_flows, 'month', split_axis=2, concat_axis=1, tiled=True)  7.56 us
    dot_general x3, matrix products, contract(): lax.dot_general(flows[leg_index], discount, (((0,), (0,)), ((), ())), pre...  7.31 us
  transfers between devices with their start and end apart: 2, of which 1 were waited for; matrix products, arithmetic and copies ran while one was open for 17% of the time, Pallas kernels for 0%

commit v1 on v0

--- a/solution.py
+++ b/solution.py
@@ -9,6 +9,28 @@
 risk_price = 0.15
 price_scale = risk_price * math.sqrt(12.0)
 price_drift = 0.5 * risk_price * risk_price
+
+
+def cut_along(x, dim, size):
+    before, after = (x.shape[:dim], x.shape[dim + 1 :])
+    return jnp.moveaxis(x.reshape(*before, size, -1, *after), dim, 0)
+
+
+def in_order(pieces, dim):
+    pieces = jnp.moveaxis(pieces, 0, dim)
+    dims = pieces.shape
+    return pieces.reshape(*dims[:dim], dims[dim] * dims[dim + 1], *dims[dim + 2 :])
+
+
+def swapped_with_each(array, axis, split_dim, concat_dim):
+    peers, mine = (lax.axis_size(axis), lax.axis_index(axis))
+    blocks = cut_along(array, split_dim, peers)
+    outs = [blocks[mine]]
+    for step in range(1, peers):
+        sent = blocks[mine ^ step]
+        outs.append(lax.ppermute(sent, axis, [(i, i ^ step) for i in range(peers)]))
+    blocks = jnp.stack(outs)[mine ^ jnp.arange(peers)]
+    return in_order(blocks, concat_dim)
 
 
 def prefix(part, axis, combine, identity):
@@ -70,7 +92,7 @@
 
 
 def local(shocks, long_mean, reversion, volatility, start_rate, cash_flows):
-    own_flows = lax.all_to_all(cash_flows, "month", split_axis=2, concat_axis=1, tiled=True)
+    own_flows = swapped_with_each(cash_flows, "month", 2, 1)
     discount = time_discount(shocks, long_mean, reversion, volatility, start_rate)
     every_month = lax.all_gather(discount, "month", axis=0, tiled=True)
     return contract(own_flows, every_month)

time: 277 us -> 195 us (0.70)
  the two profiles are of different devices: /device:TPU:0 before, /device:TPU:11 now
where the time goes in v1:
time: 195 us
  blocking collectives  74.4 us (38%)
  waiting for transfers between devices  36.2 us (19%)
  starting transfers between devices  28.1 us (14%)
  local copies, waits for them, and re-layouts  25.8 us (13%)
  between operations  14.5 us (7%)
  other arithmetic  7.72 us (4%)
  matrix products  7.49 us (4%)
    all_gather x4, blocking collectives, prefix(): gathered = jax.tree.map(lambda a: lax.all_gather(a, axis), part)  74.4 us
    ppermute x15, waiting for transfers between devices, swapped_with_each(): outs.append(lax.ppermute(sent, axis, [(i, i ^ step) for i in range(peers)]))  36.2 us
    ppermute x15, starting transfers between devices, swapped_with_each(): outs.append(lax.ppermute(sent, axis, [(i, i ^ step) for i in range(peers)]))  28.1 us
    unnamed x43, local copies, waits for them, and re-layouts  12.8 us
    dot_general x3, matrix products, contract(): lax.dot_general(flows[leg_index], discount, (((0,), (0,)), ((), ())), pre...  7.49 us
    another operation x2, local copies, waits for them, and re-layouts  6.94 us
    another operation x1, other arithmetic, contract(): return jnp.stack(blocks)  4.12 us
  transfers between devices with their start and end apart: 16, of which 8 were waited for; matrix products, arithmetic and copies ran while one was open for 12% of the time, Pallas kernels for 0%

profile of v1, /device:TPU:11, one launch (start us, length us, event | category | flops | bytes accessed | tf_op | source)
XLA Modules:
  0.0 194.6 jit_solution(13780195377608200824)
XLA Ops:
  6.5 0.7 multiply_add_fusion.13
  7.3 1.1 multiply_add_fusion.3
  11.3 19.7 %all-gather.2 = f32[16,1,2048]{2,1,0:T(1,128)S(1)} all-gather(f32[1,1,2048]{2,1,0:T(1,128)S(1)} %add_bitcast_fusion.1), channel_id=1, replica_groups=mesh['groups'=2,'month'=16] {'month'}, dimensions={0}, use_global_device_ids=true | all-gather | bytes 139264 | tf_op jit(solution)/shard_map/all_gather | solution.py:38
  31.2 17.8 %all-gather.3 = f32[16,1,2048]{2,1,0:T(1,128)S(1)} all-gather(f32[1,1,2048]{2,1,0:T(1,128)S(1)} %add_bitcast_fusion), channel_id=1, replica_groups=mesh['groups'=2,'month'=16] {'month'}, dimensions={0}, use_global_device_ids=true | all-gather | bytes 139264 | tf_op jit(solution)/shard_map/all_gather | solution.py:38
  49.1 19.1 %all-gather.1 = f32[16,1,2048]{2,1,0:T(1,128)S(1)} all-gather(f32[1,1,2048]{2,1,0:T(1,128)S(1)} %get-tuple-element.148), channel_id=1, replica_groups=mesh['groups'=2,'month'=16] {'month'}, dimensions={0}, use_global_device_ids=true | all-gather | bytes 139264 | tf_op jit(solution)/shard_map/all_gather | solution.py:38
  68.3 17.8 %all-gather = f32[16,1,2048]{2,1,0:T(1,128)S(1)} all-gather(f32[1,1,2048]{2,1,0:T(1,128)S(1)} %get-tuple-element.149), channel_id=1, replica_groups=mesh['groups'=2,'month'=16] {'month'}, dimensions={0}, use_global_device_ids=true | all-gather | bytes 139264 | tf_op jit(solution)/shard_map/all_gather | solution.py:38
  86.2 0.7 while.16
  86.9 0.7 exponential_convert_fusion
  87.7 2.2 %copy.27 = bf16[12,8,16,768]{3,2,1,0:T(8,128)(2,1)S(1)} copy(bf16[12,8,16,768]{3,1,2,0:T(8,128)(2,1)} %bitcast.144) | data formatting | bytes 4718592
  90.0 6.9 %constant_dynamic-slice_fusion.4 = (bf16[3,32,1,768]{3,2,1,0:T(2,128)(2,1)S(1)}, bf16[3,32,1,768]{3,2,1,0:T(2,128)(2,1)S(1)}, bf16[3,32,1,768]{3,2,1,0:T(2,128)(...) fusion(bf16[3,32,16,768]{3,2,1,0:T(8,128)(2,1)S(1)} %bitcast.14, ...), kind=kLoop, calls=%fused_computation.134 | loop fusion | bytes 4718656 | tf_op jit(solution)/shard_map/dynamic-slice.15
  97.1 1.7 collective-permute-start.1
  99.4 2.7 %collective-permute-start.3 = (bf16[3,32,768]{2,1,0:T(8,128)(2,1)S(1)}, bf16[3,32,768]{2,1,0:T(8,128)(2,1)S(1)}, u32[]{:S(2)}, u32[]{:S(2)}) collective-permute-start(bf16[3,32,768]{2,1,0:T(8,128)(2,1)S(1)} %bitcast.172), channel_id=1, source_target_pairs={{0,4},{1,5},{2,6},{3,7},{4,0},{5,1},{6,2},{7,3},{8,12},{9,13},{10,... | collective-permute-start | bytes 442376 | tf_op jit(solution)/shard_map/ppermute | solution.py:31
  102.3 0.7 bitcast_dynamic-update-slice_fusion
  103.2 2.6 %collective-permute-start.5 = (bf16[3,32,768]{2,1,0:T(8,128)(2,1)S(1)}, bf16[3,32,768]{2,1,0:T(8,128)(2,1)S(1)}, u32[]{:S(2)}, u32[]{:S(2)}) collective-permute-start(bf16[3,32,768]{2,1,0:T(8,128)(2,1)S(1)} %bitcast.175), channel_id=1, source_target_pairs={{0,6},{1,7},{2,4},{3,5},{4,2},{5,3},{6,0},{7,1},{8,14},{9,15},{10,... | collective-permute-start | bytes 442376 | tf_op jit(solution)/shard_map/ppermute | solution.py:31
  105.9 0.7 bitcast_dynamic-update-slice_fusion.15
  106.5 1.6 collective-permute-start.6
  108.1 0.7 bitcast_dynamic-update-slice_fusion.14
  108.8 1.3 collective-permute-start.7
  110.1 0.7 bitcast_dynamic-update-slice_fusion.13
  111.2 0.7 bitcast_dynamic-update-slice_fusion.12
  111.8 6.4 %collective-permute-done.4 = bf16[3,32,768]{2,1,0:T(8,128)(2,1)S(1)} collective-permute-done((bf16[3,32,768]{2,1,0:T(8,128)(2,1)S(1)}, bf16[3,32,768]{2,1,0:T(8,128)(2,1)S(1)}, u32[]{:S(2)}, u32[]{:S(2)}) %collective-permute-start.4) | collective-permute-done | bytes 147488 | tf_op jit(solution)/shard_map/ppermute | solution.py:31
  118.3 5.4 %collective-permute-start.9 = (bf16[3,32,768]{2,1,0:T(8,128)(2,1)S(1)}, bf16[3,32,768]{2,1,0:T(8,128)(2,1)S(1)}, u32[]{:S(2)}, u32[]{:S(2)}) collective-permute-start(bf16[3,32,768]{2,1,0:T(8,128)(2,1)S(1)} %bitcast.167), channel_id=1, source_target_pairs={{0,10},{1,11},{2,8},{3,9},{4,14},{5,15},{6,12},{7,13},{8,2},{9,3},... | collective-permute-start | bytes 442376 | tf_op jit(solution)/shard_map/ppermute | solution.py:31
  123.7 0.7 bitcast_dynamic-update-slice_fusion.11
  124.4 1.1 collective-permute-done.5
  125.5 5.5 %collective-permute-start.10 = (bf16[3,32,768]{2,1,0:T(8,128)(2,1)S(1)}, bf16[3,32,768]{2,1,0:T(8,128)(2,1)S(1)}, u32[]{:S(2)}, u32[]{:S(2)}) collective-permute-start(bf16[3,32,768]{2,1,0:T(8,128)(2,1)S(1)} %bitcast.166), channel_id=1, source_target_pairs={{0,11},{1,10},{2,9},{3,8},{4,15},{5,14},{6,13},{7,12},{8,3},{9,2},... | collective-permute-start | bytes 442376 | tf_op jit(solution)/shard_map/ppermute | solution.py:31
  131.7 1.2 collective-permute-start.11
  133.6 1.7 collective-permute-start.12
  135.9 1.5 collective-permute-start.13
  137.5 0.7 bitcast_dynamic-update-slice_fusion.7
  138.1 12.6 %collective-permute-done.9 = bf16[3,32,768]{2,1,0:T(8,128)(2,1)S(1)} collective-permute-done((bf16[3,32,768]{2,1,0:T(8,128)(2,1)S(1)}, bf16[3,32,768]{2,1,0:T(8,128)(2,1)S(1)}, u32[]{:S(2)}, u32[]{:S(2)}) %collective-permute-start.9) | collective-permute-done | bytes 147488 | tf_op jit(solution)/shard_map/ppermute | solution.py:31
  150.7 1.6 collective-permute-start.14
  152.3 0.7 bitcast_dynamic-update-slice_fusion.6
  153.0 0.9 collective-permute-done.10
  153.9 0.7 bitcast_dynamic-update-slice_fusion.5
  154.5 6.8 %collective-permute-done.11 = bf16[3,32,768]{2,1,0:T(8,128)(2,1)S(1)} collective-permute-done((bf16[3,32,768]{2,1,0:T(8,128)(2,1)S(1)}, bf16[3,32,768]{2,1,0:T(8,128)(2,1)S(1)}, u32[]{:S(2)}, u32[]{:S(2)}) %collective-permute-start.11) | collective-permute-done | bytes 147488 | tf_op jit(solution)/shard_map/ppermute | solution.py:31
  161.3 0.7 bitcast_dynamic-update-slice_fusion.4
  162.0 2.5 %collective-permute-done.12 = bf16[3,32,768]{2,1,0:T(8,128)(2,1)S(1)} collective-permute-done((bf16[3,32,768]{2,1,0:T(8,128)(2,1)S(1)}, bf16[3,32,768]{2,1,0:T(8,128)(2,1)S(1)}, u32[]{:S(2)}, u32[]{:S(2)}) %collective-permute-start.12) | collective-permute-done | bytes 147488 | tf_op jit(solution)/shard_map/ppermute | solution.py:31
  164.5 0.7 bitcast_dynamic-update-slice_fusion.3
  165.1 3.4 %collective-permute-done.13 = bf16[3,32,768]{2,1,0:T(8,128)(2,1)S(1)} collective-permute-done((bf16[3,32,768]{2,1,0:T(8,128)(2,1)S(1)}, bf16[3,32,768]{2,1,0:T(8,128)(2,1)S(1)}, u32[]{:S(2)}, u32[]{:S(2)}) %collective-permute-start.13) | collective-permute-done | bytes 147488 | tf_op jit(solution)/shard_map/ppermute | solution.py:31
  168.6 0.7 bitcast_dynamic-update-slice_fusion.2
  169.2 2.5 %collective-permute-done.14 = bf16[3,32,768]{2,1,0:T(8,128)(2,1)S(1)} collective-permute-done((bf16[3,32,768]{2,1,0:T(8,128)(2,1)S(1)}, bf16[3,32,768]{2,1,0:T(8,128)(2,1)S(1)}, u32[]{:S(2)}, u32[]{:S(2)}) %collective-permute-start.14) | collective-permute-done | bytes 147488 | tf_op jit(solution)/shard_map/ppermute | solution.py:31
  171.7 0.7 bitcast_dynamic-update-slice_fusion.1
  172.4 2.4 %gather_fusion = bf16[16,3,32,768]{3,2,1,0:T(8,128)(2,1)S(1)} fusion(bf16[16,3,32,768]{3,2,1,0:T(8,128)(2,1)} %bitcast_dynamic-update-slice_fusion.1, s32[1024]{0:T(1024)S(1)} %pad_clamp_fusion), kind=kCustom, calls=%fused_computation | custom fusion | bytes 4718656 | tf_op jit(solution)/shard_map/gather | solution.py:32
  174.8 1.3 fusion.19
  176.1 3.8 %fusion.2 = bf16[1,768,2048]{2,1,0:T(8,128)(2,1)S(1)} fusion(bf16[512,768]{1,0:T(8,128)(2,1)} %bitcast.151, bf16[512,2048]{1,0:T(8,128)(2,1)} %all-gather.6.cloned.1.call-done), kind=kOutput, calls=%fused_computation.14 | convolution fusion | flops 1612185600 | bytes 6029312 | tf_op jit(solution)/shard_map/dot_general | solution.py:87
  179.9 1.8 fusion
  181.8 1.8 fusion.1
  183.6 4.1 %pad_maximum_fusion = bf16[3,768,2048]{2,1,0:T(8,128)(2,1)} fusion(bf16[1,768,2048]{2,1,0:T(8,128)(2,1)S(1)} %fusion.2, bf16[1,768,2048]{2,1,0:T(8,128)(2,1)S(1)} %fusion.1, bf16[1,768,2048]{2,1,0:T(8,128)(2,1)S(1)} %fusion), kind=kLoop, calls=%fused_computation.8 | loop fusion | flops 9437184 | bytes 18874368 | tf_op jit(solution)/shard_map/stack | solution.py:91
  (164 shorter events, 6.6 us)
Async XLA Ops:
  6.5 169.5 %all-gather.6.cloned.1.call-start = ((), (), s32[]{:S(2)}) async-start(), calls=%async_computation | async-start | bytes 2228224 | tf_op jit(solution)/shard_map/all_gather | solution.py:97
  11.3 75.6 %copy-start.1 = (f32[2048]{0:T(1024)S(1)}, f32[2048]{0:T(1024)}, u32[]{:S(2)}) copy-start(f32[2048]{0:T(1024)} %param.12) | copy-start | bytes 24580
  97.0 6.3 %collective-permute-start = (bf16[3,32,768]{2,1,0:T(8,128)(2,1)S(1)}, bf16[3,32,768]{2,1,0:T(8,128)(2,1)S(1)}, u32[]{:S(2)}, u32[]{:S(2)}) collective-permute-start(bf16[3,32,768]{2,1,0:T(8,128)(2,1)S(1)} %bitcast.176), channel_id=1, source_target_pairs={{0,1},{1,0},{2,3},{3,2},{4,5},{5,4},{6,7},{7,6},{8,9},{9,8},{10,11... | collective-permute-start | bytes 442376 | tf_op jit(solution)/shard_map/ppermute | solution.py:31
  97.1 9.4 %collective-permute-start.1 = (bf16[3,32,768]{2,1,0:T(8,128)(2,1)S(1)}, bf16[3,32,768]{2,1,0:T(8,128)(2,1)S(1)}, u32[]{:S(2)}, u32[]{:S(2)}) collective-permute-start(bf16[3,32,768]{2,1,0:T(8,128)(2,1)S(1)} %bitcast.174), channel_id=1, source_target_pairs={{0,2},{1,3},{2,0},{3,1},{4,6},{5,7},{6,4},{7,5},{8,10},{9,11},{10,... | collective-permute-start | bytes 442376 | tf_op jit(solution)/shard_map/ppermute | solution.py:31
  98.8 10.0 %collective-permute-start.2 = (bf16[3,32,768]{2,1,0:T(8,128)(2,1)S(1)}, bf16[3,32,768]{2,1,0:T(8,128)(2,1)S(1)}, u32[]{:S(2)}, u32[]{:S(2)}) collective-permute-start(bf16[3,32,768]{2,1,0:T(8,128)(2,1)S(1)} %bitcast.173), channel_id=1, source_target_pairs={{0,3},{1,2},{2,1},{3,0},{4,7},{5,6},{6,5},{7,4},{8,11},{9,10},{10,... | collective-permute-start | bytes 442376 | tf_op jit(solution)/shard_map/ppermute | solution.py:31
  99.4 11.4 %collective-permute-start.3 = (bf16[3,32,768]{2,1,0:T(8,128)(2,1)S(1)}, bf16[3,32,768]{2,1,0:T(8,128)(2,1)S(1)}, u32[]{:S(2)}, u32[]{:S(2)}) collective-permute-start(bf16[3,32,768]{2,1,0:T(8,128)(2,1)S(1)} %bitcast.172), channel_id=1, source_target_pairs={{0,4},{1,5},{2,6},{3,7},{4,0},{5,1},{6,2},{7,3},{8,12},{9,13},{10,... | collective-permute-start | bytes 442376 | tf_op jit(solution)/shard_map/ppermute | solution.py:31
  102.0 16.2 %collective-permute-start.4 = (bf16[3,32,768]{2,1,0:T(8,128)(2,1)S(1)}, bf16[3,32,768]{2,1,0:T(8,128)(2,1)S(1)}, u32[]{:S(2)}, u32[]{:S(2)}) collective-permute-start(bf16[3,32,768]{2,1,0:T(8,128)(2,1)S(1)} %bitcast.170), channel_id=1, source_target_pairs={{0,5},{1,4},{2,7},{3,6},{4,1},{5,0},{6,3},{7,2},{8,13},{9,12},{10,... | collective-permute-start | bytes 442376 | tf_op jit(solution)/shard_map/ppermute | solution.py:31
  103.2 22.3 %collective-permute-start.5 = (bf16[3,32,768]{2,1,0:T(8,128)(2,1)S(1)}, bf16[3,32,768]{2,1,0:T(8,128)(2,1)S(1)}, u32[]{:S(2)}, u32[]{:S(2)}) collective-permute-start(bf16[3,32,768]{2,1,0:T(8,128)(2,1)S(1)} %bitcast.175), channel_id=1, source_target_pairs={{0,6},{1,7},{2,4},{3,5},{4,2},{5,3},{6,0},{7,1},{8,14},{9,15},{10,... | collective-permute-start | bytes 442376 | tf_op jit(solution)/shard_map/ppermute | solution.py:31
  106.5 25.1 %collective-permute-start.6 = (bf16[3,32,768]{2,1,0:T(8,128)(2,1)S(1)}, bf16[3,32,768]{2,1,0:T(8,128)(2,1)S(1)}, u32[]{:S(2)}, u32[]{:S(2)}) collective-permute-start(bf16[3,32,768]{2,1,0:T(8,128)(2,1)S(1)} %bitcast.171), channel_id=1, source_target_pairs={{0,7},{1,6},{2,5},{3,4},{4,3},{5,2},{6,1},{7,0},{8,15},{9,14},{10,... | collective-permute-start | bytes 442376 | tf_op jit(solution)/shard_map/ppermute | solution.py:31
  108.8 24.8 %collective-permute-start.7 = (bf16[3,32,768]{2,1,0:T(8,128)(2,1)S(1)}, bf16[3,32,768]{2,1,0:T(8,128)(2,1)S(1)}, u32[]{:S(2)}, u32[]{:S(2)}) collective-permute-start(bf16[3,32,768]{2,1,0:T(8,128)(2,1)S(1)} %bitcast.169), channel_id=1, source_target_pairs={{0,8},{1,9},{2,10},{3,11},{4,12},{5,13},{6,14},{7,15},{8,0},{9,1},... | collective-permute-start | bytes 442376 | tf_op jit(solution)/shard_map/ppermute | solution.py:31
  110.8 25.1 %collective-permute-start.8 = (bf16[3,32,768]{2,1,0:T(8,128)(2,1)S(1)}, bf16[3,32,768]{2,1,0:T(8,128)(2,1)S(1)}, u32[]{:S(2)}, u32[]{:S(2)}) collective-permute-start(bf16[3,32,768]{2,1,0:T(8,128)(2,1)S(1)} %bitcast.168), channel_id=1, source_target_pairs={{0,9},{1,8},{2,11},{3,10},{4,13},{5,12},{6,15},{7,14},{8,1},{9,0},... | collective-permute-start | bytes 442376 | tf_op jit(solution)/shard_map/ppermute | solution.py:31
  118.3 32.4 %collective-permute-start.9 = (bf16[3,32,768]{2,1,0:T(8,128)(2,1)S(1)}, bf16[3,32,768]{2,1,0:T(8,128)(2,1)S(1)}, u32[]{:S(2)}, u32[]{:S(2)}) collective-permute-start(bf16[3,32,768]{2,1,0:T(8,128)(2,1)S(1)} %bitcast.167), channel_id=1, source_target_pairs={{0,10},{1,11},{2,8},{3,9},{4,14},{5,15},{6,12},{7,13},{8,2},{9,3},... | collective-permute-start | bytes 442376 | tf_op jit(solution)/shard_map/ppermute | solution.py:31
  125.5 28.4 %collective-permute-start.10 = (bf16[3,32,768]{2,1,0:T(8,128)(2,1)S(1)}, bf16[3,32,768]{2,1,0:T(8,128)(2,1)S(1)}, u32[]{:S(2)}, u32[]{:S(2)}) collective-permute-start(bf16[3,32,768]{2,1,0:T(8,128)(2,1)S(1)} %bitcast.166), channel_id=1, source_target_pairs={{0,11},{1,10},{2,9},{3,8},{4,15},{5,14},{6,13},{7,12},{8,3},{9,2},... | collective-permute-start | bytes 442376 | tf_op jit(solution)/shard_map/ppermute | solution.py:31
  131.7 29.6 %collective-permute-start.11 = (bf16[3,32,768]{2,1,0:T(8,128)(2,1)S(1)}, bf16[3,32,768]{2,1,0:T(8,128)(2,1)S(1)}, u32[]{:S(2)}, u32[]{:S(2)}) collective-permute-start(bf16[3,32,768]{2,1,0:T(8,128)(2,1)S(1)} %bitcast.165), channel_id=1, source_target_pairs={{0,12},{1,13},{2,14},{3,15},{4,8},{5,9},{6,10},{7,11},{8,4},{9,5},... | collective-permute-start | bytes 442376 | tf_op jit(solution)/shard_map/ppermute | solution.py:31
  133.6 30.9 %collective-permute-start.12 = (bf16[3,32,768]{2,1,0:T(8,128)(2,1)S(1)}, bf16[3,32,768]{2,1,0:T(8,128)(2,1)S(1)}, u32[]{:S(2)}, u32[]{:S(2)}) collective-permute-start(bf16[3,32,768]{2,1,0:T(8,128)(2,1)S(1)} %bitcast.164), channel_id=1, source_target_pairs={{0,13},{1,12},{2,15},{3,14},{4,9},{5,8},{6,11},{7,10},{8,5},{9,4},... | collective-permute-start | bytes 442376 | tf_op jit(solution)/shard_map/ppermute | solution.py:31
  135.9 32.6 %collective-permute-start.13 = (bf16[3,32,768]{2,1,0:T(8,128)(2,1)S(1)}, bf16[3,32,768]{2,1,0:T(8,128)(2,1)S(1)}, u32[]{:S(2)}, u32[]{:S(2)}) collective-permute-start(bf16[3,32,768]{2,1,0:T(8,128)(2,1)S(1)} %bitcast.163), channel_id=1, source_target_pairs={{0,14},{1,15},{2,12},{3,13},{4,10},{5,11},{6,8},{7,9},{8,6},{9,7},... | collective-permute-start | bytes 442376 | tf_op jit(solution)/shard_map/ppermute | solution.py:31
  150.7 21.0 %collective-permute-start.14 = (bf16[3,32,768]{2,1,0:T(8,128)(2,1)S(1)}, bf16[3,32,768]{2,1,0:T(8,128)(2,1)S(1)}, u32[]{:S(2)}, u32[]{:S(2)}) collective-permute-start(bf16[3,32,768]{2,1,0:T(8,128)(2,1)S(1)} %bitcast.162), channel_id=1, source_target_pairs={{0,15},{1,14},{2,13},{3,12},{4,11},{5,10},{6,9},{7,8},{8,7},{9,6},... | collective-permute-start | bytes 442376 | tf_op jit(solution)/shard_map/ppermute | solution.py:31
  176.1 3.8 %copy-start = (bf16[1,16,32,768]{3,2,0,1:T(8,128)(2,1)S(1)}, bf16[1,16,32,768]{3,2,0,1:T(8,128)(2,1)}, u32[]{:S(2)}) copy-start(bf16[1,16,32,768]{3,2,0,1:T(8,128)(2,1)} %get-tuple-element.93) | copy-start | bytes 2359300
  176.1 3.8 %copy-start.2 = (bf16[512,2048]{1,0:T(8,128)(2,1)S(1)}, bf16[512,2048]{1,0:T(8,128)(2,1)}, u32[]{:S(2)}) copy-start(bf16[512,2048]{1,0:T(8,128)(2,1)} %all-gather.6.cloned.1.call-done) | copy-start | bytes 6291460
Sparse Core Ops, SparseCore 0:
  87.8 61.7 all-gather.5
